TPU v7x, 512 devices: a whole 4x8x8 slice. The times are simulated.
512 devices in a mesh: row: 32 (over x, z_hi, core), col: 16 (over y, z_lo).
Axes of the slice: x: 4, y: 8, z: 8 (z_hi: 4, z_lo: 2; z = z_hi * 2 + z_lo), core: 2. Of those that a mesh axis runs over, the one named last changes fastest.
Arguments:
- hidden_input: bfloat16 [4096, 2048], P('row', 'col'), may hold values from -6 to 6
- norm_gain: float32 [2048], P('col'), may hold values from 0.5 to 1.5
- router_weight: bfloat16 [2048, 4], P('col'), may hold values from -0.25 to 0.25
- expert_in: bfloat16 [4, 2, 2048, 4096], P(None, None, 'row', 'col'), may hold values from -0.125 to 0.125
- expert_out: bfloat16 [4, 4096, 2048], P(None, 'col', 'row'), may hold values from -0.09375 to 0.09375
- adapter_down: bfloat16 [16, 2048, 16], P(None, 'col'), may hold values from -0.125 to 0.125
- adapter_up: bfloat16 [16, 16, 2048], P(None, None, 'col'), may hold values from -0.375 to 0.375
- routes: int32 [4096, 2], P('row'), may hold values from 0 to 3, all different within a row
- lengths: int32 [16], replicated, may hold values from 1 to 1024, 4096 in all
- adapter_ids: int32 [16], replicated, may hold values from 0 to 15
Outputs:
- layer_out: bfloat16 [4096, 2048], P('row', 'col')
Inputs may be any that keep to these rules, and one draw needn't show every extreme that they name: `routes`: each token names two different experts. The lengths sum to 4096.
All inputs are finite; a program needn't handle non-finite values.
Results may differ from a plain program's by a relative error of at most 0.0059.
Values may be sent and summed in bfloat16 or wider, within the bound.
A program may use at most 64 MiB of HBM per device.

v0:
```python
import jax
import jax.numpy as jnp
from jax import lax
from jax.sharding import PartitionSpec as P

D = 2048


epsilon = 1e-05
adapter_scaling_factor = 2.0


def on_device(
    hidden_input,
    norm_gain,
    router_weight,
    expert_in,
    expert_out,
    adapter_down,
    adapter_up,
    routes,
    lengths,
    adapter_ids,
):
    token_count = hidden_input.shape[0]
    experts_here = expert_in.shape[0]
    adapter_count = adapter_down.shape[0]
    rank_width = adapter_down.shape[2]
    stream = hidden_input.astype(jnp.float32)
    scaled = stream * norm_gain
    row_index = lax.axis_index("row")
    position = row_index * token_count + jnp.arange(token_count, dtype=jnp.int32)
    bounds = jnp.cumsum(lengths)
    request = jnp.sum((position[:, None] >= bounds[None, :]).astype(jnp.int32), axis=1)
    request_match = request[:, None] == jnp.arange(lengths.shape[0], dtype=jnp.int32)[None, :]
    adapter = jnp.sum(jnp.where(request_match, adapter_ids[None, :], 0), axis=1)
    selector = (adapter[:, None] == jnp.arange(adapter_count, dtype=jnp.int32)[None, :]).astype(
        jnp.float32
    )
    projected = jnp.einsum(
        "td,adr->tar", scaled, adapter_down.astype(jnp.float32), precision=lax.Precision.HIGHEST
    )
    adapter_part = jnp.sum(projected * selector[:, :, None], axis=1)
    router_part = jnp.dot(
        scaled, router_weight.astype(jnp.float32), precision=lax.Precision.HIGHEST
    )
    squares = jnp.sum(stream * stream, axis=1)
    squares, router_sum, adapter_sum = lax.psum((squares, router_part, adapter_part), "col")
    inverse = lax.rsqrt(squares / D + epsilon)
    normed = (stream * inverse[:, None] * norm_gain).astype(jnp.bfloat16)
    gathered_rows = lax.all_gather(normed, "col", axis=1, tiled=True)
    logits = inverse[:, None] * router_sum
    chosen = jnp.take_along_axis(logits, routes, axis=1)
    first_gate = jax.nn.sigmoid(chosen[:, 0] - chosen[:, 1])
    second_gate = jax.nn.sigmoid(chosen[:, 1] - chosen[:, 0])
    gate_flat = jnp.stack([first_gate, second_gate], axis=1).reshape(-1)
    flat_expert = routes.reshape(-1)
    indicator = (flat_expert[:, None] == jnp.arange(experts_here, dtype=jnp.int32)[None, :]).astype(
        jnp.int32
    )
    slot_rank = jnp.sum((jnp.cumsum(indicator, axis=0) - indicator) * indicator, axis=1)
    offsets = jnp.arange(experts_here, dtype=jnp.int32) * token_count
    slot_index = jnp.sum(indicator * offsets[None, :], axis=1) + slot_rank
    sources = jnp.repeat(gathered_rows, 2, axis=0)
    buffer = (
        jnp.zeros((experts_here * token_count, gathered_rows.shape[1]), jnp.bfloat16)
        .at[slot_index]
        .set(sources)
    )
    buffer = buffer.reshape(experts_here, token_count, gathered_rows.shape[1])
    whole_in = lax.all_gather(expert_in, "row", axis=2, tiled=True)

    def group_products(rows, weights, batched_form):
        return jnp.einsum(batched_form, rows, weights, preferred_element_type=jnp.float32)

    projections = group_products(buffer, whole_in, "gsd,gkdf->gskf")
    hidden_state = (jax.nn.silu(projections[:, :, 0]) * projections[:, :, 1]).astype(jnp.bfloat16)
    weight_piece = lax.all_gather(expert_out, "row", axis=2, tiled=True)
    output_rows = group_products(hidden_state, weight_piece, "gnd,gdi->gni")
    output_rows = output_rows.reshape(experts_here * token_count, weight_piece.shape[2])
    picked = jnp.take(output_rows, slot_index, axis=0) * gate_flat[:, None]
    partial_sum_rows = jnp.sum(picked.reshape(token_count, 2, weight_piece.shape[2]), axis=1)
    mixture = lax.psum_scatter(partial_sum_rows, "col", scatter_dimension=1, tiled=True)
    latent = inverse[:, None] * adapter_sum
    spread = (selector[:, :, None] * latent[:, None, :]).reshape(
        token_count, adapter_count * rank_width
    )
    up_matrix = adapter_up.astype(jnp.float32).reshape(
        adapter_count * rank_width, adapter_up.shape[2]
    )
    adapter_delta = jnp.dot(spread, up_matrix, precision=lax.Precision.HIGHEST)
    return (mixture + adapter_scaling_factor * adapter_delta).astype(jnp.bfloat16)


def solution(mesh):
    placed = (
        P("row", "col"),
        P("col"),
        P("col", None),
        P(None, None, "row", "col"),
        P(None, "col", "row"),
        P(None, "col", None),
        P(None, None, "col"),
        P("row", None),
        P(),
        P(),
    )
    return jax.shard_map(
        on_device, mesh=mesh, in_specs=placed, out_specs=P("row", "col"), check_vma=False
    )
```

profile of v0, /device:TPU:2, one launch (start us, length us, event | category | flops | bytes accessed | tf_op | source)
XLA Modules:
  0.0 273.7 jit_solution(9909738128497496611)
XLA Ops:
  6.5 0.0 copy-start
  6.5 0.0 all-gather.3.cloned.1.call-start
  6.5 0.7 all-gather.3.cloned.1.call-update
  7.3 0.0 all-gather.5.cloned.1.call-start
  7.3 0.7 all-gather.5.cloned.1.call-update
  8.0 0.0 reduce-scatter.2.cloned.1.call-start
  8.1 0.8 copy.53
  8.8 0.1 eq.59
  9.0 0.1 eq.55
  9.1 1.2 reduce-window.18
  10.4 0.1 slice.30
  10.4 0.1 copy.55
  10.6 0.1 copy.56
  10.7 0.7 copy.65
  11.5 0.1 reduce
  11.6 0.1 convert_reduce_fusion
  11.7 0.7 select_reduce_fusion
  12.4 0.9 fusion.13
  13.3 0.0 copy-done
  13.3 1.0 fusion.11
  14.3 0.9 fusion.12
  15.2 65.5 %all-reduce = (f32[128]{0:T(128)S(1)}, f32[128,4]{0,1:T(4,128)S(1)}, f32[128,16]{0,1:T(8,128)S(1)}) all-reduce(f32[128]{0:T(128)S(1)} %fusion.13, f32[128,4]{0,1:T(4,128)S(1)} %fusion.12, f32[128,16]{0,1:T(8,128)S(1)} %multiply_reduce_fusion.1), channel_id=1, replica_groups=mesh['row'=32,'col'=16] {'col'}, use_global_device_ids=true, to_apply=%region_5.6 | all-reduce | flops 2688 | bytes 21504 | tf_op jit(solution)/shard_map/psum | solution.py:48
  80.8 0.8 fusion.15
  81.6 0.0 copy-start.1
  81.7 39.2 %all_gather.9 = bf16[128,2048]{1,0:T(8,128)(2,1)S(1)} all-gather(bf16[128,128]{1,0:T(8,128)(2,1)S(1)} %fusion.15), channel_id=1, replica_groups=mesh['row'=32,'col'=16] {'col'}, dimensions={1}, use_global_device_ids=true | all-gather | bytes 557056 | tf_op jit(solution)/shard_map/all_gather | solution.py:51
  120.8 0.6 broadcast_in_dim.29
  121.5 0.4 reshape.163
  121.9 0.0 copy-done.1
  121.9 0.1 copy.62
  122.0 0.1 reshape.153
  122.2 2.4 gather_fusion.1
  124.6 0.1 reshape.156
  124.7 0.1 copy.63
  124.8 0.1 copy.64
  125.0 0.1 add_bitcast_fusion
  125.0 0.1 fusion.23
  125.1 0.1 add.91
  125.3 0.1 copy.57
  125.3 0.1 copy.60
  125.5 3.0 %scatter_custom_fusion = bf16[512,2048]{1,0:T(8,128)(2,1)S(1)} fusion(s32[256]{0:T(256)S(1)} %bitcast.70, bf16[256,2048]{1,0:T(8,128)(2,1)S(1)} %reshape.163, bf16[]{:T(256)} %constant.35.clone.1), kind=kCustom, calls=%fused_computation.8 | custom fusion | bytes 2097154 | tf_op jit(solution)/shard_map/scatter | solution.py:68
  128.5 0.0 all-gather.3.cloned.1.call-done
  128.6 4.7 %fusion.25 = f32[4,128,2,256]{3,1,2,0:T(8,128)S(1)} fusion(bf16[4,128,2048,1]{2,1,3,0:T(8,128)(2,1)S(1)} %bitcast.66, bf16[4,2,2048,256]{3,2,1,0:T(8,128)(2,1)} %all-gather.3.cloned.1.call-done), kind=kOutput, calls=%fused_computation.59 | convolution fusion | flops 1073741824 | bytes 11534336 | tf_op jit(solution)/shard_map/gsd,gkdf->gskf/dot_general | solution.py:74
  133.2 39.7 %all-gather.5.cloned.1.call-done = bf16[4,256,2048]{1,2,0:T(8,128)(2,1)} async-done(((bf16[4,256,64]{1,2,0:T(8,128)(2,1)}), bf16[4,256,2048]{1,2,0:T(8,128)(2,1)}) %all-gather.5.cloned.1.call-update) | async-done | bytes 4194320 | tf_op jit(solution)/shard_map/all_gather | solution.py:78
  172.9 5.6 %fusion.7 = f32[4,128,2048]{2,1,0:T(8,128)} fusion(bf16[4,256,2048]{1,2,0:T(8,128)(2,1)} %all-gather.5.cloned.1.call-done, f32[4,128,2,256]{3,1,2,0:T(8,128)S(1)} %fusion.25), kind=kOutput, calls=%fused_computation.14 | convolution fusion | flops 537657344 | bytes 9437184 | tf_op jit(solution)/shard_map/gnd,gdi->gni/dot_general | solution.py:74
  178.5 4.6 %gather_fusion = f32[256,2048]{1,0:T(8,128)S(1)} fusion(f32[512,2048]{1,0:T(8,128)} %bitcast.65, s32[1024]{0:T(1024)S(1)} %pad_clamp_fusion), kind=kCustom, calls=%fused_computation | custom fusion | bytes 4195328 | tf_op jit(solution)/shard_map/jit(_take)/gather | solution.py:81
  183.1 2.3 gather.11
  185.4 0.0 copy-start.2
  185.4 6.5 %multiply_reduce_fusion = f32[128,2048]{1,0:T(8,128)} fusion(f32[128,2,2048]{2,1,0:T(2,128)} %gather.11, pred[128,2]{1,0:T(8,128)(4,1)S(1)} %copy.60, f32[128,2]{1,0:T(8,128)S(1)} %copy.64), kind=kLoop, calls=%fused_computation.3 | loop fusion | flops 1310720 | bytes 3147008 | tf_op jit(solution)/shard_map/reduce_sum | solution.py:82
  191.9 0.0 reduce-scatter.2.cloned.1.call-update
  191.9 73.5 %reduce-scatter.2.cloned.1.call-done = f32[128,128]{1,0:T(8,128)} async-done(((f32[128,2048]{1,0:T(8,128)}), f32[128,128]{1,0:T(8,128)}) %reduce-scatter.2.cloned.1.call-update) | async-done | bytes 65552 | tf_op jit(solution)/shard_map/reduce_scatter | solution.py:83
  265.4 0.0 copy-done.2
  265.5 1.7 fusion.2
  (19 shorter events, 0.2 us)
Async XLA Ops:
  6.5 6.8 %copy-start = (bf16[16,128,16]{1,2,0:T(8,128)(2,1)S(1)}, bf16[16,128,16]{1,2,0:T(8,128)(2,1)}, u32[]{:S(2)}) copy-start(bf16[16,128,16]{1,2,0:T(8,128)(2,1)} %param.15) | copy-start | bytes 196612
  6.5 122.0 %all-gather.3.cloned.1.call-start = ((), (), s32[]{:S(2)}) async-start(), calls=%async_computation.1 | async-start | bytes 8650752 | tf_op jit(solution)/shard_map/all_gather | solution.py:71
  7.3 165.6 %all-gather.5.cloned.1.call-start = ((), (), s32[]{:S(2)}) async-start(), calls=%async_computation.2 | async-start | bytes 4325376 | tf_op jit(solution)/shard_map/all_gather | solution.py:78
  8.0 257.4 %reduce-scatter.2.cloned.1.call-start = ((), (), s32[]{:S(2)}) async-start(), calls=%async_computation.3 | async-start | bytes 1114112 | tf_op jit(solution)/shard_map/reduce_scatter | solution.py:83
  81.6 40.3 %copy-start.1 = (s32[128,2]{0,1:T(2,128)S(1)}, s32[128,2]{0,1:T(2,128)}, u32[]{:S(2)}) copy-start(s32[128,2]{0,1:T(2,128)} %param.17) | copy-start | bytes 3076
  185.4 80.1 %copy-start.2 = (bf16[16,16,128]{2,1,0:T(8,128)(2,1)S(1)}, bf16[16,16,128]{2,1,0:T(8,128)(2,1)}, u32[]{:S(2)}) copy-start(bf16[16,16,128]{2,1,0:T(8,128)(2,1)} %param.16) | copy-start | bytes 196612
Sparse Core Ops, SparseCore 0:
  10.6 96.6 all-gather.2
  110.6 62.3 all-gather.4
  192.1 73.3 reduce-scatter.1
where the time goes:
time: 274 us
  waiting for transfers between devices  115 us (42%)
  blocking collectives  105 us (38%)
  local copies, waits for them, and re-layouts  16.3 us (6%)
  matrix products  13.9 us (5%)
  between operations  13.3 us (5%)
  other arithmetic  10.8 us (4%)
    reduce_scatter x1, waiting for transfers between devices, on_device(): lax.psum_scatter(partial_sum_rows, 'col', scatter_dimension=1, tiled=True)  73.5 us
    psum x1, blocking collectives, on_device(): lax.psum((squares, router_part, adapter_part), 'col')  65.5 us
    all_gather x1, waiting for transfers between devices, on_device(): weight_piece = lax.all_gather(expert_out, 'row', axis=2, tiled=True)  39.7 us
    all_gather x1, blocking collectives, on_device(): gathered_rows = lax.all_gather(normed, 'col', axis=1, tiled=True)  39.2 us
    dot_general x2, matrix products, group_products(): jnp.einsum(batched_form, rows, weights, preferred_element_type=jnp.float32)  10.3 us
    gather x2, local copies, waits for them, and re-layouts, on_device(): picked = jnp.take(output_rows, slot_index, axis=0) * gate_flat[:, None]  6.88 us
    reduce_sum x1, other arithmetic, on_device(): jnp.sum(picked.reshape(token_count, 2, weight_piece.shape[2]), axis=1)  6.51 us
  transfers between devices with their start and end apart: 3, of which 2 were waited for; matrix products, arithmetic and copies ran while one was open for 7% of the time, Pallas kernels for 0%

commit v1 on v0

v1 whole, which is shorter than its diff:
```python
import jax
import jax.numpy as jnp
from jax import lax
from jax.experimental import pallas as pl
from jax.experimental.pallas import tpu as pltpu
from jax.sharding import PartitionSpec as P

NX, NZ, NC = 4, 4, 16
RING = 8
B = 128
D = 2048
F = 256
SLAB = 64
RANK, ADAPTERS, REQUESTS = 16, 16, 16
epsilon = 1e-05
adapter_scaling_factor = 2.0

MESH = pl.DeviceIdType.MESH
F32, BF16 = jnp.float32, jnp.bfloat16
HIGH = lax.Precision.HIGHEST
NT = (((1,), (1,)), ((), ()))
TN = (((0,), (0,)), ((), ()))


def kernel(
    lengths, adapter_ids, h_ref, gain_ref, small_ref, up_ref, routes_ref, win_ref, wout_ref, out_ref,
    xb, nb, wb, ob, hid, pr, lr, tr, inv_b, gate_b, pstage, lstage,
    rs_send, rs_recv, sm_send, sm_recv,
    local_sem, az_s, az_r, ab_s, ab_r, wz_s, wz_r, wx_s, wx_r, wp_s, wp_r,
    p_s, p_r, l_s, l_r, t_s, t_r, rs_s, rs_r, sm_s, sm_r,
):
    row, col = lax.axis_index("row"), lax.axis_index("col")
    k = lax.rem(row, 2)
    chip_row = lax.div(row, 2)
    x, zh = lax.div(chip_row, NZ), lax.rem(chip_row, NZ)
    y, zl = lax.div(col, 2), lax.rem(col, 2)
    z = zh * 2 + zl
    big, small = y * (1 - k) + z * k, z * (1 - k) + y * k
    sy, sz = RING * (1 - k) + k, RING * k + (1 - k)

    def at_plane(b, s):
        yy, zz = b * (1 - k) + s * k, s * (1 - k) + b * k
        return ((x * NZ + lax.div(zz, 2)) * 2 + k, yy * 2 + lax.rem(zz, 2))

    def at_x(xx):
        return ((lax.rem(xx + NX, NX) * NZ + zh) * 2 + k, col)

    def ring(v):
        return lax.rem(v + RING, RING)

    pending = []

    def send(src, dst, s_sem, r_sem, device):
        copy = pltpu.make_async_remote_copy(
            src_ref=src, dst_ref=dst, send_sem=s_sem, recv_sem=r_sem, device_id=device, device_id_type=MESH
        )
        copy.start()
        pending.append(copy)

    partner = (chip_row * 2 + 1 - k, col)

    def arrived(dst, s_sem, r_sem):
        pltpu.make_async_remote_copy(
            src_ref=dst, dst_ref=dst, send_sem=s_sem, recv_sem=r_sem, device_id=partner, device_id_type=MESH
        ).wait_recv()

    peers = [(row, lax.rem(col + d, NC)) for d in range(1, NC)]
    for d in range(1, NZ):
        for e in range(2):
            peers.append(((x * NZ + lax.rem(zh + d, NZ)) * 2 + k, y * 2 + e))
    peers += [at_x(x + 1), at_x(x - 1), partner]
    barrier = pltpu.get_barrier_semaphore()
    for peer in peers:
        pl.semaphore_signal(barrier, inc=1, device_id=peer, device_id_type=MESH)
    pl.semaphore_wait(barrier, len(peers))

    mine = xb.at[big * RING + small]
    own_x = pltpu.make_async_copy(h_ref, mine, local_sem.at[0])
    own_x.start()
    for d in range(1, RING):
        send(h_ref, mine, az_s.at[d], az_r.at[d], at_plane(big, ring(small + d)))

    def rows_of(xx, jj):
        zz = lax.rem(zh - jj + NZ, NZ)
        r = (lax.rem(xx + NX, NX) * NZ + zz) * 2 + k
        return pl.ds(pl.multiple_of(r * SLAB, SLAB), SLAB)

    my_rows = rows_of(x, 0)
    own_w = [
        pltpu.make_async_copy(win_ref.at[zh], wb.at[pl.ds(0, 2), my_rows], local_sem.at[1]),
        pltpu.make_async_copy(wout_ref.at[zh], wb.at[2, my_rows], local_sem.at[2]),
    ]
    for copy in own_w:
        copy.start()
    for j in (2, 1, 3):
        e = lax.rem(zh + j, NZ)
        to = ((x * NZ + e) * 2 + k, col)
        send(win_ref.at[e], wb.at[pl.ds(0, 2), my_rows], wz_s.at[j, 0], wz_r.at[j, 0], to)
        send(wout_ref.at[e], wb.at[2, my_rows], wz_s.at[j, 1], wz_r.at[j, 1], to)

    def w_piece(xx, j):
        return wb.at[:, rows_of(xx, j)]

    def w_out(xx, j, slot, right=False, left=False):
        piece = w_piece(xx, j)
        if right:
            m = j if slot == 0 else 4 + j
            send(piece, piece, wx_s.at[0, m], wx_r.at[0, m], at_x(x + 1))
        if left:
            m = j if slot == 0 else 4 + j
            send(piece, piece, wx_s.at[1, m], wx_r.at[1, m], at_x(x - 1))
        send(piece, piece, wp_s.at[slot * 4 + j], wp_r.at[slot * 4 + j], partner)

    def w_own(j):
        if j == 0:
            for copy in own_w:
                copy.wait()
        else:
            rows = rows_of(x, j)
            arrived(wb.at[pl.ds(0, 2), rows], wz_s.at[j, 0], wz_r.at[j, 0])
            arrived(wb.at[2, rows], wz_s.at[j, 1], wz_r.at[j, 1])
        w_out(x, j, 0, right=True, left=True)

    def w_near(j):
        arrived(w_piece(x - 1, j), wx_s.at[0, j], wx_r.at[0, j])
        w_out(x - 1, j, 1, right=j < 2)
        arrived(w_piece(x + 1, j), wx_s.at[1, j], wx_r.at[1, j])
        w_out(x + 1, j, 2, left=j >= 2)

    def w_far(j):
        side = 0 if j < 2 else 1
        arrived(w_piece(x + 2, j), wx_s.at[side, 4 + j], wx_r.at[side, 4 + j])
        w_out(x + 2, j, 3)

    w_own(0)

    hx = h_ref[...].astype(F32)
    ones = jnp.ones((8, B), F32)
    squares = lax.dot_general(ones, hx * hx, NT, precision=HIGH, preferred_element_type=F32)
    projected = lax.dot_general(small_ref[...], hx, NT, precision=HIGH, preferred_element_type=F32)
    line = lax.broadcasted_iota(jnp.int32, (8, B), 0)
    tile = projected[ADAPTERS * RANK :]
    tile = jnp.where(line == 0, squares, tile)
    tile = jnp.where(line == 5, jnp.broadcast_to(gain_ref[...], (8, B)), tile)
    pstage[...] = tile
    position = row * B + lax.broadcasted_iota(jnp.int32, (1, B), 1)
    bound = lengths[0]
    request = (position >= bound).astype(jnp.int32)
    for i in range(1, REQUESTS):
        bound = bound + lengths[i]
        request = request + (position >= bound).astype(jnp.int32)
    adapter = jnp.zeros((1, B), jnp.int32)
    for i in range(REQUESTS):
        adapter = jnp.where(request == i, adapter_ids[i], adapter)
    adapter = jnp.broadcast_to(adapter, (RANK, B))
    part = jnp.zeros((RANK, B), F32)
    for a in range(ADAPTERS):
        part = part + jnp.where(adapter == a, projected[a * RANK : (a + 1) * RANK], 0.0)
    lstage[...] = part
    pr[col] = tile
    lr[col] = part
    for d in range(1, NC):
        send(pstage, pr.at[col], p_s.at[d], p_r.at[d], (row, lax.rem(col + d, NC)))

    def a_piece(b, p):
        return xb.at[pl.ds(ring(b) * RING + 4 * p, 4)]

    def a_send(step, p, way):
        b = big - (step - 1) if way == 0 else big + (step - 1)
        to = at_plane(ring(big + 1), small) if way == 0 else at_plane(ring(big - 1), small)
        m = (step - 1) * 2 + p
        send(a_piece(b, p), a_piece(b, p), ab_s.at[way, m], ab_r.at[way, m], to)

    def a_step(step):
        for p in range(2):
            for way in range(2):
                if step == 4 and p != way:
                    continue
                m = (step - 1) * 2 + p
                b = big - step if way == 0 else big + step
                arrived(a_piece(b, p), ab_s.at[way, m], ab_r.at[way, m])
                if step < 3 or (step == 3 and p == way):
                    a_send(step + 1, p, way)

    own_x.wait()
    for d in range(1, RING):
        arrived(xb.at[big * RING + ring(small - d)], az_s.at[d], az_r.at[d])
    for p in range(2):
        a_send(1, p, 0)
        a_send(1, p, 1)

    w_own(1)
    w_own(3)
    w_near(0)

    for d in range(1, NC):
        arrived(pr.at[lax.rem(col - d + NC, NC)], p_s.at[d], p_r.at[d])
    total = pr[0]
    for i in range(1, NC):
        total = total + pr[i]
    inverse = lax.rsqrt(total[0:1] / D + epsilon)
    logits = [total[1 + e : 2 + e] * inverse for e in range(NZ)]
    route = [routes_ref[0:1, :], routes_ref[1:2, :]]
    chosen = []
    for i in range(2):
        value = jnp.zeros((1, B), F32)
        for e in range(NZ):
            value = jnp.where(route[i] == e, logits[e], value)
        chosen.append(value)
    gates = [jax.nn.sigmoid(chosen[0] - chosen[1]), jax.nn.sigmoid(chosen[1] - chosen[0])]
    share = jnp.where(line == 0, jnp.broadcast_to(inverse, (8, B)), 0.0)
    for e in range(NZ):
        weight = jnp.where(route[0] == e, gates[0], 0.0) + jnp.where(route[1] == e, gates[1], 0.0)
        share = jnp.where(line == 1 + e, jnp.broadcast_to(weight, (8, B)), share)
    tr[zh] = share
    for d in range(1, NZ):
        to = ((x * NZ + lax.rem(zh + d, NZ)) * 2 + k, col)
        send(tr.at[zh], tr.at[zh], t_s.at[d], t_r.at[d], to)
    for d in range(1, NC):
        send(lstage, lr.at[col], l_s.at[d], l_r.at[d], (row, lax.rem(col + d, NC)))

    a_step(1)
    w_own(2)
    w_near(1)
    a_step(2)
    w_near(3)
    w_near(2)
    w_far(0)
    a_step(3)

    for d in range(1, NZ):
        arrived(tr.at[lax.rem(zh - d + NZ, NZ)], t_s.at[d], t_r.at[d])
    for i in range(NZ):
        rows = tr[i]
        gate_row = tr[i, pl.ds(1 + zh, 1), :]
        both = jnp.where(line == 0, rows, jnp.broadcast_to(gate_row, (8, B)))
        turned = jnp.transpose(both)
        inv_b[i] = jnp.broadcast_to(turned[:, 0:1], (B, B))
        gate_b[i] = jnp.broadcast_to(turned[:, 1:2], (B, B))

    def normalise(b):
        @pl.loop(0, RING)
        def _(s):
            yy, zz = b * (1 - k) + s * k, s * (1 - k) + b * k
            c, t = yy * 2 + lax.rem(zz, 2), lax.div(zz, 2)
            value = xb[b * RING + s].astype(F32) * inv_b[t] * pr[c, pl.ds(5, 1), :]
            nb[pl.ds(pl.multiple_of(t * B, B), B), pl.ds(pl.multiple_of(c * B, B), B)] = value.astype(BF16)

    w_far(1)
    normalise(big)
    for d in range(1, 4):
        normalise(ring(big - d))
        normalise(ring(big + d))
    w_far(3)
    w_far(2)
    a_step(4)
    normalise(ring(big + 4))
    for slot in range(4):
        xx = (x, x - 1, x + 1, x + 2)[slot]
        for j in range(4):
            zz = lax.rem(zh - j + NZ, NZ)
            r = (lax.rem(xx + NX, NX) * NZ + zz) * 2 + 1 - k
            arrived(
                wb.at[:, pl.ds(pl.multiple_of(r * SLAB, SLAB), SLAB)], wp_s.at[slot * 4 + j], wp_r.at[slot * 4 + j]
            )

    @pl.loop(0, 2)
    def _(i):
        rows = pl.ds(pl.multiple_of(i * 256, 256), 256)
        tokens = nb[rows, :]
        gate = jnp.dot(tokens, wb[0], preferred_element_type=F32)
        up = jnp.dot(tokens, wb[1], preferred_element_type=F32)
        hid[rows, :] = (jax.nn.silu(gate) * up).astype(BF16)

    @pl.loop(0, RING)
    def _(yy):
        weights = wb[2, pl.ds(pl.multiple_of(yy * 256, 256), 256), :]
        result = lax.dot_general(hid[...], weights, NT, preferred_element_type=F32)
        for t in range(NZ):
            for half in range(2):
                block = result[t * B : (t + 1) * B, half * B : (half + 1) * B]
                ob[yy * sy + (t * 2 + half) * sz] = block * gate_b[t]

    def r_send(j, p, way):
        m = (4 - j) * 2 + p
        b = ring(big + j) if way == 0 else ring(big - j)
        own = ob[pl.ds(b * RING + 4 * p, 4)]
        if j == 3 and p == way or j < 3:
            before = m - 2
            arrived(rs_recv.at[way, before], rs_s.at[way, before], rs_r.at[way, before])
            own = own + rs_recv[way, before].astype(F32)
        rs_send[way, m] = own.astype(BF16)
        to = at_plane(ring(big + 1), small) if way == 0 else at_plane(ring(big - 1), small)
        send(rs_send.at[way, m], rs_recv.at[way, m], rs_s.at[way, m], rs_r.at[way, m], to)

    r_send(4, 0, 0)
    r_send(4, 1, 1)
    r_send(3, 1, 0)
    r_send(3, 0, 1)
    r_send(3, 0, 0)
    r_send(3, 1, 1)
    for j in (2, 1):
        r_send(j, 1, 0)
        r_send(j, 0, 1)
        r_send(j, 0, 0)
        r_send(j, 1, 1)

    for d in range(1, NC):
        arrived(lr.at[lax.rem(col - d + NC, NC)], l_s.at[d], l_r.at[d])
    latent = lr[0]
    for i in range(1, NC):
        latent = latent + lr[i]
    latent = latent * jnp.broadcast_to(inverse, (RANK, B))
    spread = jnp.concatenate([jnp.where(adapter == a, latent, 0.0) for a in range(ADAPTERS)], axis=0)
    delta = lax.dot_general(spread, up_ref[...].astype(F32), TN, precision=HIGH, preferred_element_type=F32)

    for p in range(2):
        total4 = ob[pl.ds(big * RING + 4 * p, 4)]
        for way in range(2):
            m = 6 + p
            arrived(rs_recv.at[way, m], rs_s.at[way, m], rs_r.at[way, m])
            total4 = total4 + rs_recv[way, m].astype(F32)
        ob[pl.ds(big * RING + 4 * p, 4)] = total4
        sm_send[pl.ds(4 * p, 4)] = total4.astype(BF16)
    for d in range(1, RING):
        s = ring(small + d)
        send(sm_send.at[s], sm_recv.at[small], sm_s.at[d], sm_r.at[d], at_plane(big, s))
    result = ob[big * RING + small] + adapter_scaling_factor * delta
    for d in range(1, RING):
        s = ring(small - d)
        arrived(sm_recv.at[s], sm_s.at[d], sm_r.at[d])
        result = result + sm_recv[s].astype(F32)
    out_ref[...] = result.astype(BF16)
    for copy in pending:
        copy.wait_send()


def on_device(
    hidden_input, norm_gain, router_weight, expert_in, expert_out, adapter_down, adapter_up, routes, lengths, adapter_ids
):
    down = jnp.transpose(adapter_down, (0, 2, 1)).reshape(ADAPTERS * RANK, B)
    pad = jnp.zeros((1, B), BF16)
    table = jnp.concatenate([down, pad, router_weight.T, pad, pad, pad], axis=0).astype(F32) * norm_gain[None, :]
    vmem = pl.BlockSpec(memory_space=pltpu.VMEM)
    smem = pl.BlockSpec(memory_space=pltpu.SMEM)
    hbm = pl.BlockSpec(memory_space=pl.ANY)
    dma = pltpu.SemaphoreType.DMA
    return pl.pallas_call(
        kernel,
        out_shape=jax.ShapeDtypeStruct((B, B), BF16),
        in_specs=[smem, smem, vmem, vmem, vmem, vmem, vmem, hbm, hbm],
        out_specs=vmem,
        scratch_shapes=[
            pltpu.VMEM((RING * RING, B, B), BF16),
            pltpu.VMEM((NZ * B, D), BF16),
            pltpu.VMEM((3, D, F), BF16),
            pltpu.VMEM((RING * RING, B, B), F32),
            pltpu.VMEM((NZ * B, F), BF16),
            pltpu.VMEM((NC, 8, B), F32),
            pltpu.VMEM((NC, RANK, B), F32),
            pltpu.VMEM((NZ, 8, B), F32),
            pltpu.VMEM((NZ, B, B), F32),
            pltpu.VMEM((NZ, B, B), F32),
            pltpu.VMEM((8, B), F32),
            pltpu.VMEM((RANK, B), F32),
            pltpu.VMEM((2, 8, 4, B, B), BF16),
            pltpu.VMEM((2, 8, 4, B, B), BF16),
            pltpu.VMEM((RING, B, B), BF16),
            pltpu.VMEM((RING, B, B), BF16),
            dma((3,)),
            dma((RING,)), dma((RING,)),
            dma((2, 8)), dma((2, 8)),
            dma((NZ, 2)), dma((NZ, 2)),
            dma((2, 8)), dma((2, 8)),
            dma((16,)), dma((16,)),
            dma((NC,)), dma((NC,)),
            dma((NC,)), dma((NC,)),
            dma((NZ,)), dma((NZ,)),
            dma((2, 8)), dma((2, 8)),
            dma((RING,)), dma((RING,)),
        ],
        compiler_params=pltpu.CompilerParams(
            collective_id=0, has_side_effects=True, vmem_limit_bytes=48 * 1024 * 1024
        ),
    )(
        lengths, adapter_ids, hidden_input, norm_gain[None, :], table,
        adapter_up.reshape(ADAPTERS * RANK, B), routes.T, expert_in, jnp.transpose(expert_out, (0, 2, 1)),
    )


def solution(mesh):
    placed = (
        P("row", "col"),
        P("col"),
        P("col", None),
        P(None, None, "row", "col"),
        P(None, "col", "row"),
        P(None, "col", None),
        P(None, None, "col"),
        P("row", None),
        P(),
        P(),
    )
    return jax.shard_map(
        on_device, mesh=mesh, in_specs=placed, out_specs=P("row", "col"), check_vma=False
    )
```

time: 274 us -> 81.4 us (0.30)
  the two profiles are of different devices: /device:TPU:2 before, /device:TPU:8 now
where the time goes in v1:
time: 81.4 us; the launch traced here: 81.1 us
  Pallas kernels  77.6 us (95%)
  local copies, waits for them, and re-layouts  2.44 us (3%)
  other arithmetic  1.02 us (1%)
    pallas_call x1, Pallas kernels, on_device(): pl.pallas_call(kernel, out_shape=jax.ShapeDtypeStruct((B, B), BF16), in_s...  77.6 us
    unnamed x17, local copies, waits for them, and re-layouts  2.35 us

profile of v1, /device:TPU:8, one launch (start us, length us, event | category | flops | bytes accessed | tf_op | source)
XLA Modules:
  0.0 81.1 jit_solution(7818072970586261121)
XLA Ops:
  0.0 0.0 copy-start.1
  0.0 0.1 pad.3.clone
  0.1 0.0 copy-start.2
  0.1 0.0 copy-start.4
  0.1 0.0 copy-start.5
  0.1 0.0 copy-start.6
  0.1 0.0 copy-start.7
  0.1 1.0 %convert_multiply_fusion.small_ref = f32[264,128]{1,0:T(8,128)S(1)} fusion(bf16[4,128]{1,0:T(4,128)(2,1)} %bitcast.14, bf16[256,128]{1,0:T(8,128)(2,1)} %bitcast.13, f32[128]{0:T(128)} %param.11, bf16[264]{0:T(512)(128)(2,1)S(1)} %pad.3.clone, bf16[264]{0:T(512)(128)(2,1)S(1)} %pad.1.clone), kind=kLoop, calls=%fused_computation | loop fusion | flops 304128 | bytes 203296 | tf_op jit(solution)/shard_map/mul | solution.py:343
  1.2 0.0 copy-done.1
  1.2 0.0 copy-done.2
  1.2 0.0 copy-done.4
  1.2 0.0 copy-done.5
  1.2 0.0 copy-done.6
  1.2 0.0 copy-done.7
  1.2 0.0 copy-start
  1.2 0.9 %copy-done = bf16[4,2,64,256]{3,2,1,0:T(8,128)(2,1)S(1)} copy-done((bf16[4,2,64,256]{3,2,1,0:T(8,128)(2,1)S(1)}, bf16[4,2,64,256]{3,2,1,0:T(8,128)(2,1)}, u32[]{:S(2)}) %copy-start) | copy-done | bytes 262168
  2.2 0.0 copy-start.3
  2.2 0.8 copy-done.3
  2.9 77.6 %shard_map.100 = bf16[128,128]{1,0:T(8,128)(2,1)S(1)} custom-call(s32[16]{0:T(128)S(1)} %copy-done.6, s32[16]{0:T(128)S(1)} %copy-done.7, bf16[128,128]{1,0:T(8,128)(2,1)S(1)} %copy-done.3, f32[1,128]{1,0:T(1,128)S(1)} %bitcast.11, f32[264,128]{1,0:T(8,128)S(1)} %convert_multiply_fusion.small_ref, bf16[256,128]{1,0:T(8,128)(2,1)S(1)} %bitcast.10, ...), custom_call_target="tpu_custom_call" | custom-call | tf_op jit(solution)/shard_map/pallas_call | solution.py:348
  80.5 0.6 copy.12
  (2 shorter events, 0.0 us)
Async XLA Ops:
  0.0 1.2 %copy-start.1 = (bf16[4,256,64]{1,2,0:T(8,128)(2,1)S(1)}, bf16[4,256,64]{1,2,0:T(8,128)(2,1)}, u32[]{:S(2)}) copy-start(bf16[4,256,64]{1,2,0:T(8,128)(2,1)} %param.14) | copy-start | bytes 393220
  0.1 1.1 %copy-start.2 = (bf16[16,16,128]{2,1,0:T(8,128)(2,1)S(1)}, bf16[16,16,128]{2,1,0:T(8,128)(2,1)}, u32[]{:S(2)}) copy-start(bf16[16,16,128]{2,1,0:T(8,128)(2,1)} %param.16) | copy-start | bytes 196612
  0.1 1.1 %copy-start.4 = (f32[128]{0:T(128)S(1)}, f32[128]{0:T(128)}, u32[]{:S(2)}) copy-start(f32[128]{0:T(128)} %param.11) | copy-start | bytes 1540
  0.1 1.1 %copy-start.5 = (s32[128,2]{0,1:T(2,128)S(1)}, s32[128,2]{0,1:T(2,128)}, u32[]{:S(2)}) copy-start(s32[128,2]{0,1:T(2,128)} %param.17) | copy-start | bytes 3076
  0.1 1.1 %copy-start.6 = (s32[16]{0:T(128)S(1)}, s32[16]{0:T(128)}, u32[]{:S(2)}) copy-start(s32[16]{0:T(128)} %lengths.1) | copy-start | bytes 196
  0.1 1.1 %copy-start.7 = (s32[16]{0:T(128)S(1)}, s32[16]{0:T(128)}, u32[]{:S(2)}) copy-start(s32[16]{0:T(128)} %adapter_ids.1) | copy-start | bytes 196
  1.2 1.0 %copy-start = (bf16[4,2,64,256]{3,2,1,0:T(8,128)(2,1)S(1)}, bf16[4,2,64,256]{3,2,1,0:T(8,128)(2,1)}, u32[]{:S(2)}) copy-start(bf16[4,2,64,256]{3,2,1,0:T(8,128)(2,1)} %win_ref.1) | copy-start | bytes 786436
  2.2 0.8 copy-start.3

commit v2 on v0

v2 whole, which is shorter than its diff:
```python
import jax
import jax.numpy as jnp
from jax import lax
from jax.experimental import pallas as pl
from jax.experimental.pallas import tpu as pltpu
from jax.sharding import PartitionSpec as P

NX, NZ, NC = 4, 4, 16
RING = 8
B = 128
D = 2048
F = 256
SLAB = 64
RANK, ADAPTERS, REQUESTS = 16, 16, 16
A_TWO = (5, 6, 7)
O_TWO = ()
FAR = (2,)
A_READY = (0.0, 4.0, 4.1, 5.0, 5.1, 6.5, 6.6, 8.0)
W_READY = (0.0, 8.5, 14.0, 9.0)
O_RING_AT = ((11.1, 7.4, 3.7, -2.0), (7.4, 3.7, -2.0))
O_TWO_AT = ((5.0, 6.0, 0.7, 0.5), (5.0, 6.0, 0.6))
O_LAST_AT = (15.0, 12.6)
O_SPREAD = 0.1
epsilon = 1e-05
adapter_scaling_factor = 2.0

MESH = pl.DeviceIdType.MESH
F32, BF16 = jnp.float32, jnp.bfloat16
HIGH = lax.Precision.HIGHEST
NT = (((1,), (1,)), ((), ()))
TN = (((0,), (0,)), ((), ()))


def kernel(
    lengths_hbm, ids_hbm, h_hbm, gain_hbm, router_hbm, down_hbm, up_hbm, routes_hbm, win_ref, wout_ref, out_ref,
    lengths, adapter_ids, h_ref, gain_ref, router_ref, down_ref, up_ref, routes_ref,
    xb, nb, wb, ob, hid, pr, pz, tr, inv_b, gate_b, pstage,
    rs_send, rs_recv, sm_send, sm_recv,
    acc, local_sem, sent, az_r, ab_r, wz_r, wx_r, wp_r, p_r, pz_r, t_r, rs_r, sm_r,
):
    row, col = lax.axis_index("row"), lax.axis_index("col")
    k = lax.rem(row, 2)
    chip_row = lax.div(row, 2)
    x, zh = lax.div(chip_row, NZ), lax.rem(chip_row, NZ)
    y, zl = lax.div(col, 2), lax.rem(col, 2)
    z = zh * 2 + zl
    big, small = y * (1 - k) + z * k, z * (1 - k) + y * k
    sy, sz = RING * (1 - k) + k, RING * k + (1 - k)

    def at_plane(b, s):
        yy, zz = b * (1 - k) + s * k, s * (1 - k) + b * k
        return ((x * NZ + lax.div(zz, 2)) * 2 + k, yy * 2 + lax.rem(zz, 2))

    def at_x(xx):
        return ((lax.rem(xx + NX, NX) * NZ + zh) * 2 + k, col)

    def ring(v):
        return lax.rem(v + RING, RING)

    partner = (chip_row * 2 + 1 - k, col)

    def send(src, dst, group, r_sem, device):
        pltpu.make_async_remote_copy(
            src_ref=src, dst_ref=dst, send_sem=sent.at[group], recv_sem=r_sem, device_id=device, device_id_type=MESH
        ).start()

    def waiter(ref, group, r_sem):
        return pltpu.make_async_remote_copy(
            src_ref=ref, dst_ref=ref, send_sem=sent.at[group], recv_sem=r_sem, device_id=partner, device_id_type=MESH
        )

    def arrived(dst, r_sem):
        waiter(dst, 0, r_sem).wait_recv()

    def rows_of(xx, jj):
        zz = lax.rem(zh - jj + NZ, NZ)
        r = (lax.rem(xx + NX, NX) * NZ + zz) * 2 + k
        return pl.ds(pl.multiple_of(r * SLAB, SLAB), SLAB)

    my_rows = rows_of(x, 0)
    mine = xb.at[big * RING + small]
    own_w = [
        pltpu.make_async_copy(win_ref.at[zh], wb.at[pl.ds(0, 2), my_rows], local_sem.at[1]),
        pltpu.make_async_copy(wout_ref.at[zh], wb.at[2, my_rows], local_sem.at[2]),
    ]
    blocks = [
        pltpu.make_async_copy(src, dst, local_sem.at[3 + i])
        for i, (src, dst) in enumerate((
            (h_hbm, h_ref), (gain_hbm, gain_ref), (router_hbm, router_ref), (down_hbm, down_ref),
            (lengths_hbm, lengths), (ids_hbm, adapter_ids), (routes_hbm, routes_ref), (up_hbm, up_ref),
        ))
    ]
    own_x = pltpu.make_async_copy(h_hbm, mine, local_sem.at[0])
    for copy in own_w + blocks + [own_x]:
        copy.start()

    peers = [at_plane(ring(big + d), small) for d in range(1, RING)]
    peers += [at_plane(big, ring(small + d)) for d in range(1, RING)]
    peers += [at_x(x + d) for d in range(1, NX)] + [partner]
    barrier = pltpu.get_barrier_semaphore()
    for peer in peers:
        pl.semaphore_signal(barrier, inc=1, device_id=peer, device_id_type=MESH)
    pl.semaphore_wait(barrier, len(peers))

    offsets = (0, 1, -1, 2, -2, 3, -3, 4)

    def a_block(b, offset):
        return xb.at[ring(b) * RING + ring(small - offset)]

    def a_long_send(i, start, way, to_distance):
        b = big - start if way == 0 else big + start
        ahead = to_distance - start
        to = at_plane(ring(big + ahead), small) if way == 0 else at_plane(ring(big - ahead), small)
        dst = a_block(b, offsets[i])
        src = h_hbm if i == 0 and start == 0 else dst
        send(src, dst, 1, ab_r.at[way, i, to_distance - 1], to)

    def onward(two, i, way, d):
        last = 4 if i % 2 == way else 3
        if two:
            served = {0: (1, 2), 2: (3, 4)}.get(d, ())
        else:
            served = (d + 1,)
        return [v for v in served if v <= last]

    def a_long(i, d, way):
        b = big - d if way == 0 else big + d
        if d:
            arrived(a_block(b, offsets[i]), ab_r.at[way, i, d - 1])
        for v in onward(i in A_TWO, i, way, d):
            a_long_send(i, d, way, v)

    def a_short(i):
        arrived(a_block(big, offsets[i]), az_r.at[i])
        for w in range(2):
            a_long(i, 0, w)

    for i in range(1, RING):
        send(h_hbm, mine, 0, az_r.at[i], at_plane(big, ring(small + offsets[i])))
    for w in range(2):
        a_long(0, 0, w)

    for j in (1, 3, 2):
        e = lax.rem(zh + j, NZ)
        to = ((x * NZ + e) * 2 + k, col)
        send(win_ref.at[e], wb.at[pl.ds(0, 2), my_rows], 2, wz_r.at[j], to)
        send(wout_ref.at[e], wb.at[2, my_rows], 2, wz_r.at[j], to)

    def w_piece(xx, j):
        return wb.at[:, rows_of(xx, j)]

    def w_out(xx, j, slot, right=False, left=False, far=False):
        piece = w_piece(xx, j)
        if right:
            m = j if slot == 0 else 4 + j
            send(piece, piece, 3, wx_r.at[0, m], at_x(x + 1))
        if left:
            m = j if slot == 0 else 4 + j
            send(piece, piece, 3, wx_r.at[1, m], at_x(x - 1))
        if far:
            side = 0 if j < 2 else 1
            send(piece, piece, 3, wx_r.at[side, 4 + j], at_x(x + 2))
        send(piece, piece, 4, wp_r.at[slot // 3], partner)

    def w_own(j):
        if j == 0:
            for copy in own_w:
                copy.wait()
        else:
            arrived(w_piece(x, j), wz_r.at[j])
        w_out(x, j, 0, right=True, left=True, far=j in FAR)

    def w_near(j, way):
        if way == 0:
            arrived(w_piece(x - 1, j), wx_r.at[0, j])
            w_out(x - 1, j, 1, right=j < 2 and j not in FAR)
        else:
            arrived(w_piece(x + 1, j), wx_r.at[1, j])
            w_out(x + 1, j, 2, left=j >= 2 and j not in FAR)

    def w_far(j):
        side = 0 if j < 2 else 1
        arrived(w_piece(x + 2, j), wx_r.at[side, 4 + j])
        w_out(x + 2, j, 3)

    w_own(0)

    for copy in blocks:
        copy.wait()
    hx = h_ref[...].astype(F32)
    ones = jnp.ones((8, B), F32)
    squares = lax.dot_general(ones, hx * hx, NT, precision=HIGH, preferred_element_type=F32)
    scaled = hx * gain_ref[...]
    projected = lax.dot_general(down_ref[...].astype(F32), scaled, NT, precision=HIGH, preferred_element_type=F32)
    routed = lax.dot_general(router_ref[...].astype(F32), scaled, NT, precision=HIGH, preferred_element_type=F32)
    line = lax.broadcasted_iota(jnp.int32, (8, B), 0)
    tile = squares
    for e in range(NZ):
        tile = jnp.where(line == 1 + e, jnp.broadcast_to(routed[e : e + 1], (8, B)), tile)
    tile = jnp.where(line >= 5, 0.0, tile)
    tile = jnp.where(line == 5 + zl, jnp.broadcast_to(gain_ref[...], (8, B)), tile)
    position = row * B + lax.broadcasted_iota(jnp.int32, (1, B), 1)
    bound = lengths[0]
    request = (position >= bound).astype(jnp.int32)
    for i in range(1, REQUESTS):
        bound = bound + lengths[i]
        request = request + (position >= bound).astype(jnp.int32)
    adapter = jnp.zeros((1, B), jnp.int32)
    for i in range(REQUESTS):
        adapter = jnp.where(request == i, adapter_ids[i], adapter)
    adapter = jnp.broadcast_to(adapter, (RANK, B))
    part = jnp.zeros((RANK, B), F32)
    for a in range(ADAPTERS):
        part = part + jnp.where(adapter == a, projected[a * RANK : (a + 1) * RANK], 0.0)
    pstage[0, 0:8] = tile
    pstage[0, 8:24] = part
    other = (row, y * 2 + 1 - zl)
    send(pstage.at[0], pz, 6, pz_r.at[0], other)

    def pair_event():
        arrived(pz, pz_r.at[0])
        both = pz[...] + jnp.concatenate([tile, part], axis=0)
        pstage[1] = both
        pr[y] = both
        for d in range(1, RING):
            send(pstage.at[1], pr.at[y], 5, p_r.at[0], (row, ring(y + d) * 2 + zl))

    def gates_event():
        arrived(pr.at[pl.ds(0, RING - 1)], p_r.at[0])
        total = pr[0]
        for i in range(1, RING):
            total = total + pr[i]
        inverse = lax.rsqrt(total[0:1] / D + epsilon)
        logits = [total[1 + e : 2 + e] * inverse for e in range(NZ)]
        route = [routes_ref[0:1, :], routes_ref[1:2, :]]
        chosen = []
        for i in range(2):
            value = jnp.zeros((1, B), F32)
            for e in range(NZ):
                value = jnp.where(route[i] == e, logits[e], value)
            chosen.append(value)
        gates = [jax.nn.sigmoid(chosen[0] - chosen[1]), jax.nn.sigmoid(chosen[1] - chosen[0])]
        share = jnp.where(line == 0, jnp.broadcast_to(inverse, (8, B)), 0.0)
        for e in range(NZ):
            weight = jnp.where(route[0] == e, gates[0], 0.0) + jnp.where(route[1] == e, gates[1], 0.0)
            share = jnp.where(line == 1 + e, jnp.broadcast_to(weight, (8, B)), share)
        tr[zh] = share
        for d in range(1, NZ):
            to = ((x * NZ + lax.rem(zh + d, NZ)) * 2 + k, col)
            send(tr.at[zh], tr.at[zh], 7, t_r.at[0], to)
        return inverse, total[8:24] * jnp.broadcast_to(inverse, (RANK, B))

    def columns_event():
        arrived(tr.at[pl.ds(0, NZ - 1)], t_r.at[0])
        for i in range(NZ):
            rows = tr[i]
            gate_row = tr[i, pl.ds(1 + zh, 1), :]
            both = jnp.where(line == 0, rows, jnp.broadcast_to(gate_row, (8, B)))
            turned = jnp.transpose(both)
            inv_b[i] = jnp.broadcast_to(turned[:, 0:1], (B, B))
            gate_b[i] = jnp.broadcast_to(turned[:, 1:2], (B, B))

    events = [(5.0, pair_event, ()), (11.0, gates_event, ()), (16.0, columns_event, ())]
    for i in range(RING):
        ready = A_READY[i]
        if i:
            events.append((ready, a_short, (i,)))
        for way in range(2):
            for d in range(1, 5 if i % 2 == way else 4):
                hops = ((d + 1) // 2 if i in A_TWO else d)
                events.append((ready + 3.5 * hops, a_long, (i, d, way)))
    for j, ready in enumerate(W_READY):
        for way in range(2):
            events.append((ready + 4.0, w_near, (j, way)))
        if j:
            events.append((ready, w_own, (j,)))
        events.append((ready + (5.0 if j in FAR else 8.0), w_far, (j,)))
    kept = {}
    for _, action, given in sorted(events, key=lambda event: event[0]):
        kept[action] = action(*given)
    latent = kept[gates_event][1]
    own_x.wait()

    @pl.loop(0, RING * RING)
    def _(i):
        yy, zz = lax.div(i, RING), lax.rem(i, RING)
        c, t = yy * 2 + lax.rem(zz, 2), lax.div(zz, 2)
        value = xb[yy * sy + zz * sz].astype(F32) * inv_b[t] * pr[yy, pl.ds(5 + lax.rem(zz, 2), 1), :]
        nb[pl.ds(pl.multiple_of(t * B, B), B), pl.ds(pl.multiple_of(c * B, B), B)] = value.astype(BF16)

    def contract(step, xx):
        part = pl.ds(pl.multiple_of(lax.rem(xx + NX, NX) * 512, 512), 512)

        @pl.loop(0, 2)
        def _(i):
            rows = pl.ds(pl.multiple_of(i * 256, 256), 256)
            tokens = nb[rows, part]
            sums = [jnp.dot(tokens, wb[n, part, :], preferred_element_type=F32) for n in range(2)]
            if step:
                sums = [acc[n, rows, :] + sums[n] for n in range(2)]
            if step < 3:
                for n in range(2):
                    acc[n, rows, :] = sums[n]
            else:
                hid[rows, :] = (jax.nn.silu(sums[0]) * sums[1]).astype(BF16)

    arrived(wb.at[:, pl.ds(0, 12 * SLAB)], wp_r.at[0])
    for step in range(3):
        contract(step, (x, x - 1, x + 1)[step])
    arrived(wb.at[:, pl.ds(0, 4 * SLAB)], wp_r.at[1])
    contract(3, x + 2)

    @pl.loop(0, RING)
    def _(yy):
        weights = wb[2, pl.ds(pl.multiple_of(yy * 256, 256), 256), :]
        result = lax.dot_general(hid[...], weights, NT, preferred_element_type=F32)
        for t in range(NZ):
            for half in range(2):
                block = result[t * B : (t + 1) * B, half * B : (half + 1) * B]
                ob[yy * sy + (t * 2 + half) * sz] = block * gate_b[t]

    targets = (4, 3, -3, 2, -2, 1, -1, 0)

    def r_sum(i, j, way, value):
        arrived(rs_recv.at[(way * RING + i) * 4 + j - 1], rs_r.at[way, i, j - 1])
        return value + rs_recv[(way * RING + i) * 4 + j - 1].astype(F32)

    def r_send(i, j, way):
        b = ring(big + j) if way == 0 else ring(big - j)
        value = ob[b * RING + ring(small + targets[i])]
        last = 4 if i % 2 == way else 3
        if i in O_TWO:
            sources = [v for v in (3, 4) if v <= last] if j == 2 else []
            ahead = {1: 1, 2: 2, 3: 1, 4: 2}[j]
        else:
            sources = [j + 1] if j < last else []
            ahead = 1
        for v in sources:
            value = r_sum(i, v, way, value)
        rs_send[(way * RING + i) * 4 + j - 1] = value.astype(BF16)
        to = at_plane(ring(big + ahead), small) if way == 0 else at_plane(ring(big - ahead), small)
        send(rs_send.at[(way * RING + i) * 4 + j - 1], rs_recv.at[(way * RING + i) * 4 + j - 1], 8, rs_r.at[way, i, j - 1], to)

    def r_last(i):
        s = ring(small + targets[i])
        value = ob[big * RING + s]
        for way in range(2):
            for v in (1, 2) if i in O_TWO else (1,):
                value = r_sum(i, v, way, value)
        if targets[i]:
            sm_send[i] = value.astype(BF16)
            send(sm_send.at[i], sm_recv.at[i], 9, sm_r.at[0], at_plane(big, s))
        return value

    def delta_event():
        spread = jnp.concatenate([jnp.where(adapter == a, latent, 0.0) for a in range(ADAPTERS)], axis=0)
        delta = lax.dot_general(spread, up_ref[...].astype(F32), TN, precision=HIGH, preferred_element_type=F32)
        return delta

    events = [(7.0, delta_event, ())]
    for i in range(RING):
        for way in range(2):
            first = 4 if i % 2 == way else 3
            for j in range(1, first + 1):
                when = (O_TWO_AT if i in O_TWO else O_RING_AT)[first == 3][j - 1] + O_SPREAD * i
                events.append((when, r_send, (i, j, way)))
        events.append((O_LAST_AT[i in O_TWO] + O_SPREAD * i, r_last, (i,)))
    for _, action, given in sorted(events, key=lambda event: event[0]):
        kept[action] = action(*given)
    result = kept[r_last] + adapter_scaling_factor * kept[delta_event]
    arrived(sm_recv.at[pl.ds(0, RING - 1)], sm_r.at[0])
    for i in range(RING - 1):
        result = result + sm_recv[i].astype(F32)
    out_ref[...] = result.astype(BF16)
    for group, ref in enumerate((
        xb.at[pl.ds(0, 7)], xb.at[pl.ds(0, 56)], wb.at[:, pl.ds(0, 3 * SLAB)], wb.at[:, pl.ds(0, 12 * SLAB)],
        wb.at[:, pl.ds(0, 16 * SLAB)], pr.at[pl.ds(0, 7)], pz, tr.at[pl.ds(0, 3)],
        rs_send.at[pl.ds(0, 56)], sm_send.at[pl.ds(0, 7)],
    )):
        waiter(ref, group, pz_r.at[0]).wait_send()


def on_device(
    hidden_input, norm_gain, router_weight, expert_in, expert_out, adapter_down, adapter_up, routes, lengths, adapter_ids
):
    down = jnp.transpose(adapter_down, (0, 2, 1)).reshape(ADAPTERS * RANK, B)
    vmem = pl.BlockSpec(memory_space=pltpu.VMEM)
    hbm = pl.BlockSpec(memory_space=pltpu.HBM)
    dma = pltpu.SemaphoreType.DMA
    return pl.pallas_call(
        kernel,
        out_shape=jax.ShapeDtypeStruct((B, B), BF16),
        in_specs=[hbm] * 10,
        out_specs=vmem,
        scratch_shapes=[
            pltpu.SMEM((REQUESTS,), jnp.int32),
            pltpu.SMEM((REQUESTS,), jnp.int32),
            pltpu.VMEM((B, B), BF16),
            pltpu.VMEM((1, B), F32),
            pltpu.VMEM((NZ, B), BF16),
            pltpu.VMEM((ADAPTERS * RANK, B), BF16),
            pltpu.VMEM((ADAPTERS * RANK, B), BF16),
            pltpu.VMEM((2, B), jnp.int32),
            pltpu.VMEM((RING * RING, B, B), BF16),
            pltpu.VMEM((NZ * B, D), BF16),
            pltpu.VMEM((3, D, F), BF16),
            pltpu.VMEM((RING * RING, B, B), F32),
            pltpu.VMEM((NZ * B, F), BF16),
            pltpu.VMEM((RING, 24, B), F32),
            pltpu.VMEM((24, B), F32),
            pltpu.VMEM((NZ, 8, B), F32),
            pltpu.VMEM((NZ, B, B), F32),
            pltpu.VMEM((NZ, B, B), F32),
            pltpu.VMEM((2, 24, B), F32),
            pltpu.VMEM((8 * RING, B, B), BF16),
            pltpu.VMEM((8 * RING, B, B), BF16),
            pltpu.VMEM((RING, B, B), BF16),
            pltpu.VMEM((RING, B, B), BF16),
            pltpu.VMEM((2, NZ * B, F), F32),
            dma((11,)),
            dma((10,)),
            dma((RING,)),
            dma((2, RING, 4)),
            dma((NZ,)),
            dma((2, 8)),
            dma((2,)),
            dma((1,)), dma((1,)), dma((1,)),
            dma((2, RING, 4)),
            dma((1,)),
        ],
        compiler_params=pltpu.CompilerParams(
            collective_id=0, has_side_effects=True
        ),
    )(
        lengths, adapter_ids, hidden_input, norm_gain[None, :], router_weight.T, down,
        adapter_up.reshape(ADAPTERS * RANK, B), routes.T, expert_in, jnp.transpose(expert_out, (0, 2, 1)),
    )


def solution(mesh):
    placed = (
        P("row", "col"),
        P("col"),
        P("col", None),
        P(None, None, "row", "col"),
        P(None, "col", "row"),
        P(None, "col", None),
        P(None, None, "col"),
        P("row", None),
        P(),
        P(),
    )
    return jax.shard_map(
        on_device, mesh=mesh, in_specs=placed, out_specs=P("row", "col"), check_vma=False
    )
```

time: 274 us -> 77.2 us (0.28)
  waiting for transfers between devices: 115 us -> 0 us
  blocking collectives: 105 us -> 0 us
  Pallas kernels: 0 us -> 75.7 us
  local copies, waits for them, and re-layouts: 16.3 us -> 1.38 us
  matrix products: 13.9 us -> 0 us
  between operations: 13.3 us -> 0.01 us
  other arithmetic: 10.8 us -> 0 us
    pallas_call x0 -> x1, Pallas kernels: none -> 75.7 us  [on_device(): pl.pallas_call(kernel, out_shape=jax.ShapeDtypeStruct((B, B), BF16), in_s...]
    reduce_scatter x1 -> x0, waiting for transfers between devices: 73.5 us -> none  [on_device(): lax.psum_scatter(partial_sum_rows, 'col', scatter_dimension=1, tiled=True)]
    psum x1 -> x0, blocking collectives: 65.5 us -> none  [on_device(): lax.psum((squares, router_part, adapter_part), 'col')]
    all_gather x2 -> x0, waiting for transfers between devices: 39.7 us -> none  [the longest x1 39.7 us: on_device(): weight_piece = lax.all_gather(expert_out, 'row', axis=2, tiled=True)]
    all_gather x1 -> x0, blocking collectives: 39.2 us -> none  [on_device(): gathered_rows = lax.all_gather(normed, 'col', axis=1, tiled=True)]
    dot_general x4 -> x0, matrix products: 12.9 us -> none  [the longest x2 10.3 us: group_products(): jnp.einsum(batched_form, rows, weights, preferred_element_type=jnp.float32)]
    gather x7 -> x0, local copies, waits for them, and re-layouts: 9.7 us -> none  [the longest x2 6.88 us: on_device(): picked = jnp.take(output_rows, slot_index, axis=0) * gate_flat[:, None]]
    reduce_sum x6 -> x0, other arithmetic: 8.32 us -> none  [the longest x1 6.51 us: on_device(): jnp.sum(picked.reshape(token_count, 2, weight_piece.shape[2]), axis=1)]
  transfers between devices with their start and end apart: 3 -> 0, of which waited for: 2 -> 0; matrix products, arithmetic and copies ran while one was open for 7% -> 0% of each run, Pallas kernels for 0% -> 0%
where the time goes in v2:
time: 77.2 us; the launch traced here: 77.1 us
  Pallas kernels  75.7 us (98%)
  local copies, waits for them, and re-layouts  1.38 us (2%)
    pallas_call x1, Pallas kernels, on_device(): pl.pallas_call(kernel, out_shape=jax.ShapeDtypeStruct((B, B), BF16), in_s...  75.7 us

profile of v2, /device:TPU:2, one launch (start us, length us, event | category | flops | bytes accessed | tf_op | source)
XLA Modules:
  0.0 77.1 jit_solution(17597945796813075592)
XLA Ops:
  0.0 75.7 %shard_map.100 = bf16[128,128]{1,0:T(8,128)(2,1)} custom-call(s32[16]{0:T(128)} %lengths_hbm.1, s32[16]{0:T(128)} %ids_hbm.1, bf16[128,128]{1,0:T(8,128)(2,1)} %h_hbm.1, f32[1,128]{1,0:T(1,128)} %bitcast.13, bf16[4,128]{1,0:T(4,128)(2,1)} %bitcast.11, bf16[256,128]{1,0:T(8,128)(2,1)} %bitcast.9, bf16[256,128]{1,0:T(8,128)(2,1)} %bitcast.10, ...), custom_call_target="tpu_custom_call" | custom-call | tf_op jit(solution)/shard_map/pallas_call | solution.py:390
  75.7 1.4 %copy.12 = bf16[128,128]{1,0:T(8,128)(2,1)} copy(bf16[128,128]{1,0:T(8,128)(2,1)} %shard_map.100) | data formatting | bytes 65536

commit v3 on v2

--- a/solution.py
+++ b/solution.py
@@ -15,12 +15,15 @@
 A_TWO = (5, 6, 7)
 O_TWO = ()
 FAR = (2,)
-A_READY = (0.0, 4.0, 4.1, 5.0, 5.1, 6.5, 6.6, 8.0)
+A_READY = (0.0, 5.0, 5.1, 6.0, 6.1, 7.0, 7.1, 8.5)
 W_READY = (0.0, 8.5, 14.0, 9.0)
 O_RING_AT = ((11.1, 7.4, 3.7, -2.0), (7.4, 3.7, -2.0))
 O_TWO_AT = ((5.0, 6.0, 0.7, 0.5), (5.0, 6.0, 0.6))
 O_LAST_AT = (15.0, 12.6)
 O_SPREAD = 0.1
+P_AT = (9.0, 17.0, 26.0)
+A_HOP = 3.9
+W_AFTER = (4.0, 5.0, 8.0)
 epsilon = 1e-05
 adapter_scaling_factor = 2.0
 
@@ -260,7 +263,7 @@
             inv_b[i] = jnp.broadcast_to(turned[:, 0:1], (B, B))
             gate_b[i] = jnp.broadcast_to(turned[:, 1:2], (B, B))
 
-    events = [(5.0, pair_event, ()), (11.0, gates_event, ()), (16.0, columns_event, ())]
+    events = [(P_AT[0], pair_event, ()), (P_AT[1], gates_event, ()), (P_AT[2], columns_event, ())]
     for i in range(RING):
         ready = A_READY[i]
         if i:
@@ -268,13 +271,13 @@
         for way in range(2):
             for d in range(1, 5 if i % 2 == way else 4):
                 hops = ((d + 1) // 2 if i in A_TWO else d)
-                events.append((ready + 3.5 * hops, a_long, (i, d, way)))
+                events.append((ready + A_HOP * hops, a_long, (i, d, way)))
     for j, ready in enumerate(W_READY):
         for way in range(2):
-            events.append((ready + 4.0, w_near, (j, way)))
+            events.append((ready + W_AFTER[0], w_near, (j, way)))
         if j:
             events.append((ready, w_own, (j,)))
-        events.append((ready + (5.0 if j in FAR else 8.0), w_far, (j,)))
+        events.append((ready + (W_AFTER[1] if j in FAR else W_AFTER[2]), w_far, (j,)))
     kept = {}
     for _, action, given in sorted(events, key=lambda event: event[0]):
         kept[action] = action(*given)

time: 77.2 us -> 73.7 us (0.955)
  the two profiles are of different devices: /device:TPU:2 before, /device:TPU:4 now
where the time goes in v3:
time: 73.7 us; the launch traced here: 73.5 us
  Pallas kernels  72.1 us (98%)
  local copies, waits for them, and re-layouts  1.38 us (2%)
    pallas_call x1, Pallas kernels, on_device(): pl.pallas_call(kernel, out_shape=jax.ShapeDtypeStruct((B, B), BF16), in_s...  72.1 us

profile of v3, /device:TPU:4, one launch (start us, length us, event | category | flops | bytes accessed | tf_op | source)
XLA Modules:
  0.0 73.5 jit_solution(7310719302978288488)
XLA Ops:
  0.0 72.1 %shard_map.100 = bf16[128,128]{1,0:T(8,128)(2,1)} custom-call(s32[16]{0:T(128)} %lengths_hbm.1, s32[16]{0:T(128)} %ids_hbm.1, bf16[128,128]{1,0:T(8,128)(2,1)} %h_hbm.1, f32[1,128]{1,0:T(1,128)} %bitcast.13, bf16[4,128]{1,0:T(4,128)(2,1)} %bitcast.11, bf16[256,128]{1,0:T(8,128)(2,1)} %bitcast.9, bf16[256,128]{1,0:T(8,128)(2,1)} %bitcast.10, ...), custom_call_target="tpu_custom_call" | custom-call | tf_op jit(solution)/shard_map/pallas_call | solution.py:393
  72.1 1.4 %copy.12 = bf16[128,128]{1,0:T(8,128)(2,1)} copy(bf16[128,128]{1,0:T(8,128)(2,1)} %shard_map.100) | data formatting | bytes 65536

commit v4 on v3

--- a/solution.py
+++ b/solution.py
@@ -13,13 +13,13 @@
 SLAB = 64
 RANK, ADAPTERS, REQUESTS = 16, 16, 16
 A_TWO = (5, 6, 7)
-O_TWO = ()
+O_TWO = (0, 1, 2)
 FAR = (2,)
 A_READY = (0.0, 5.0, 5.1, 6.0, 6.1, 7.0, 7.1, 8.5)
 W_READY = (0.0, 8.5, 14.0, 9.0)
 O_RING_AT = ((11.1, 7.4, 3.7, -2.0), (7.4, 3.7, -2.0))
-O_TWO_AT = ((5.0, 6.0, 0.7, 0.5), (5.0, 6.0, 0.6))
-O_LAST_AT = (15.0, 12.6)
+O_TWO_AT = ((8.3, 5.8, 0.7, 0.5), (8.3, 5.8, 0.6))
+O_LAST_AT = (15.0, 13.2)
 O_SPREAD = 0.1
 P_AT = (9.0, 17.0, 26.0)
 A_HOP = 3.9
@@ -294,9 +294,9 @@
     def contract(step, xx):
         part = pl.ds(pl.multiple_of(lax.rem(xx + NX, NX) * 512, 512), 512)
 
-        @pl.loop(0, 2)
+        @pl.loop(0, 1)
         def _(i):
-            rows = pl.ds(pl.multiple_of(i * 256, 256), 256)
+            rows = pl.ds(pl.multiple_of(i * 512, 512), 512)
             tokens = nb[rows, part]
             sums = [jnp.dot(tokens, wb[n, part, :], preferred_element_type=F32) for n in range(2)]
             if step:

time: 73.7 us -> 72.3 us (0.981)
  the two profiles are of different devices: /device:TPU:4 before, /device:TPU:2 now
where the time goes in v4:
time: 72.3 us; the launch traced here: 72.2 us
  Pallas kernels  70.8 us (98%)
  local copies, waits for them, and re-layouts  1.38 us (2%)
    pallas_call x1, Pallas kernels, on_device(): pl.pallas_call(kernel, out_shape=jax.ShapeDtypeStruct((B, B), BF16), in_s...  70.8 us

profile of v4, /device:TPU:2, one launch (start us, length us, event | category | flops | bytes accessed | tf_op | source)
XLA Modules:
  0.0 72.2 jit_solution(5021425085266139034)
XLA Ops:
  0.0 70.8 %shard_map.100 = bf16[128,128]{1,0:T(8,128)(2,1)} custom-call(s32[16]{0:T(128)} %lengths_hbm.1, s32[16]{0:T(128)} %ids_hbm.1, bf16[128,128]{1,0:T(8,128)(2,1)} %h_hbm.1, f32[1,128]{1,0:T(1,128)} %bitcast.13, bf16[4,128]{1,0:T(4,128)(2,1)} %bitcast.11, bf16[256,128]{1,0:T(8,128)(2,1)} %bitcast.9, bf16[256,128]{1,0:T(8,128)(2,1)} %bitcast.10, ...), custom_call_target="tpu_custom_call" | custom-call | tf_op jit(solution)/shard_map/pallas_call | solution.py:393
  70.8 1.4 %copy.12 = bf16[128,128]{1,0:T(8,128)(2,1)} copy(bf16[128,128]{1,0:T(8,128)(2,1)} %shard_map.100) | data formatting | bytes 65536

commit v5 on v4

--- a/solution.py
+++ b/solution.py
@@ -291,27 +291,11 @@
         value = xb[yy * sy + zz * sz].astype(F32) * inv_b[t] * pr[yy, pl.ds(5 + lax.rem(zz, 2), 1), :]
         nb[pl.ds(pl.multiple_of(t * B, B), B), pl.ds(pl.multiple_of(c * B, B), B)] = value.astype(BF16)
 
-    def contract(step, xx):
-        part = pl.ds(pl.multiple_of(lax.rem(xx + NX, NX) * 512, 512), 512)
-
-        @pl.loop(0, 1)
-        def _(i):
-            rows = pl.ds(pl.multiple_of(i * 512, 512), 512)
-            tokens = nb[rows, part]
-            sums = [jnp.dot(tokens, wb[n, part, :], preferred_element_type=F32) for n in range(2)]
-            if step:
-                sums = [acc[n, rows, :] + sums[n] for n in range(2)]
-            if step < 3:
-                for n in range(2):
-                    acc[n, rows, :] = sums[n]
-            else:
-                hid[rows, :] = (jax.nn.silu(sums[0]) * sums[1]).astype(BF16)
-
     arrived(wb.at[:, pl.ds(0, 12 * SLAB)], wp_r.at[0])
-    for step in range(3):
-        contract(step, (x, x - 1, x + 1)[step])
     arrived(wb.at[:, pl.ds(0, 4 * SLAB)], wp_r.at[1])
-    contract(3, x + 2)
+    gate = jnp.dot(nb[...], wb[0], preferred_element_type=F32)
+    up = jnp.dot(nb[...], wb[1], preferred_element_type=F32)
+    hid[...] = (jax.nn.silu(gate) * up).astype(BF16)
 
     @pl.loop(0, RING)
     def _(yy):

time: 72.3 us -> 72.3 us (level)
  no operation moved by 1% of the time
where the time goes in v5:
time: 72.3 us; the launch traced here: 72.1 us
  Pallas kernels  70.7 us (98%)
  local copies, waits for them, and re-layouts  1.38 us (2%)
    pallas_call x1, Pallas kernels, on_device(): pl.pallas_call(kernel, out_shape=jax.ShapeDtypeStruct((B, B), BF16), in_s...  70.7 us

profile of v5, /device:TPU:2, one launch (start us, length us, event | category | flops | bytes accessed | tf_op | source)
XLA Modules:
  0.0 72.1 jit_solution(4397895762559801209)
XLA Ops:
  0.0 70.7 %shard_map.100 = bf16[128,128]{1,0:T(8,128)(2,1)} custom-call(s32[16]{0:T(128)} %lengths_hbm.1, s32[16]{0:T(128)} %ids_hbm.1, bf16[128,128]{1,0:T(8,128)(2,1)} %h_hbm.1, f32[1,128]{1,0:T(1,128)} %bitcast.13, bf16[4,128]{1,0:T(4,128)(2,1)} %bitcast.11, bf16[256,128]{1,0:T(8,128)(2,1)} %bitcast.9, bf16[256,128]{1,0:T(8,128)(2,1)} %bitcast.10, ...), custom_call_target="tpu_custom_call" | custom-call | tf_op jit(solution)/shard_map/pallas_call | solution.py:377
  70.7 1.4 %copy.12 = bf16[128,128]{1,0:T(8,128)(2,1)} copy(bf16[128,128]{1,0:T(8,128)(2,1)} %shard_map.100) | data formatting | bytes 65536
